TPU v7x, 32 devices: a whole 2x2x4 slice. The times are simulated.
32 devices in a mesh: clips: 16 (over z, x, core), mlp: 2 (over y).
Axes of the slice: x: 2, y: 2, z: 4, core: 2. Of those that a mesh axis runs over, the one named last changes fastest.
Arguments:
- flat_params: bfloat16 [3804160], replicated
- w_fc1: bfloat16 [768, 3072], P(None, 'mlp'), may hold values from -0.21875 to 0.21875
- w_fc2: bfloat16 [3072, 768], P('mlp'), may hold values from -0.15625 to 0.15625
- w_up: bfloat16 [512, 2048], P(None, 'mlp'), may hold values from -0.25 to 0.25
- w_down: bfloat16 [2048, 512], P('mlp'), may hold values from -0.21875 to 0.21875
- patches: bfloat16 [9984, 768], P(('clips', 'mlp')), may hold values from -6 to 6
- clip_ids: int32 [49152], P(('clips', 'mlp')), may hold values from 0 to 2, as said below
- visible_index: int32 [9984], P(('clips', 'mlp')), may hold values from 0 to 1535, as said below
- cotangent: bfloat16 [49152, 512], P(('clips', 'mlp')), may hold values from -6 to 6
Outputs:
- decoded: bfloat16 [49152, 512], P(('clips', 'mlp'))
- input_grad: float32 [9984, 768], P(('clips', 'mlp'))
- param_grad: float32 [3804160], P('mlp')
- fc1_grad: float32 [768, 3072], P(None, 'mlp')
- fc2_grad: float32 [3072, 768], P('mlp')
- up_grad: float32 [512, 2048], P(None, 'mlp')
- down_grad: float32 [2048, 512], P('mlp')
Inputs may be any that keep to these rules, and one draw needn't show every extreme that they name: `clip_ids`: each buffer of 1536 patches is either one clip of 192 x 8 patches, all with id 0, or three clips of 512 patches with ids 0, 1, 2 in order; a clip's patch (t, f) is row t * 8 + f of it. Both kinds occur in every draw. `visible_index`: the 312 entries of a buffer are distinct and increasing positions within that buffer; a three-clip buffer has 104 of them in each clip.
All inputs are finite; a program needn't handle non-finite values.
Results may differ from a plain program's by a relative error of at most 0.028.
Values may be sent and summed in bfloat16 or wider, within the bound.
No kernel may reach another device: no remote copies, remote signals or barrier semaphores. Data moves between devices by JAX's collectives and lax.ppermute only.
A program may use at most 384 MiB of HBM per device.

v0:
```python
import math
import jax
import jax.numpy as jnp
from jax import lax
from jax.sharding import PartitionSpec as P

D = 768
HEADS = 12
DD = 512
DHEADS = 16
FREQ = 8
WIN = 4
LONG_FRAMES = 192
ROWS = 1536
VIS = 312
PARAMS = 3804160
EPSILON = 1e-06


def layer_norm(inputs, weight_gain):
    row_mean = jnp.mean(inputs, axis=-1, keepdims=True)
    centred = inputs - row_mean
    variance = jnp.mean(centred * centred, axis=-1, keepdims=True)
    return centred * lax.rsqrt(variance + EPSILON) * weight_gain


def exact_gelu(inputs):
    return jax.nn.gelu(inputs, approximate=False)


def unpack(flat):
    layout = ((D, 3 * D), (D, D), (D,), (D,), (D, DD), (DD,), (DD, 3 * DD), (DD, DD), (DD,), (DD,))
    members = []
    offset = 0
    for dims_of in layout:
        length = math.prod(dims_of)
        members.append(flat[offset : offset + length].reshape(dims_of))
        offset = offset + length
    return members


def to_windows(source, head_count):
    head_size = source.shape[-1] // head_count
    blocks = source.reshape(-1, LONG_FRAMES // WIN, WIN, FREQ // WIN, WIN, head_count, head_size)
    blocks = blocks.transpose(0, 1, 3, 2, 4, 5, 6)
    return blocks.reshape(-1, WIN * WIN, head_count, head_size)


def from_windows(source, buffers):
    blocks = source.reshape(buffers, LONG_FRAMES // WIN, FREQ // WIN, WIN, WIN, -1)
    blocks = blocks.transpose(0, 1, 3, 2, 4, 5)
    return blocks.reshape(buffers * ROWS, -1)


def matmul(left, right):
    return jnp.dot(left, right, preferred_element_type=jnp.float32)


def transposed(left, right):
    return lax.dot_general(
        left, right, (((0,), (0,)), ((), ())), preferred_element_type=jnp.float32
    )


def against(left, right):
    return lax.dot_general(
        left, right, (((1,), (1,)), ((), ())), preferred_element_type=jnp.float32
    )


def score_table(queries, key_rows, allowed):
    factor = 1.0 / math.sqrt(queries.shape[-1])
    scores = (
        jnp.einsum("bqhd,bkhd->bhqk", queries, key_rows, preferred_element_type=jnp.float32)
        * factor
    )
    if allowed is not None:
        scores = jnp.where(allowed, scores, -1e30)
    return scores


def attend_forward(queries, key_rows, val_rows, allowed):
    scores = score_table(queries, key_rows, allowed)
    highest = jnp.max(scores, axis=-1, keepdims=True)
    expont = jnp.exp(scores - highest)
    total_row = jnp.sum(expont, axis=-1, keepdims=True)
    attn_probs = (expont / total_row).astype(jnp.bfloat16)
    mixed = jnp.einsum("bhqk,bkhd->bqhd", attn_probs, val_rows, preferred_element_type=jnp.float32)
    return (mixed, highest + jnp.log(total_row))


def attend_backward(queries, key_rows, val_rows, allowed, log_total, mix_grad):
    factor = 1.0 / math.sqrt(queries.shape[-1])
    attn_probs = jnp.exp(score_table(queries, key_rows, allowed) - log_total)
    prob_grad = jnp.einsum(
        "bqhd,bkhd->bhqk", mix_grad, val_rows, preferred_element_type=jnp.float32
    )
    score_grad = (
        attn_probs * (prob_grad - jnp.sum(attn_probs * prob_grad, axis=-1, keepdims=True))
    ).astype(jnp.bfloat16)
    query_grad = (
        jnp.einsum("bhqk,bkhd->bqhd", score_grad, key_rows, preferred_element_type=jnp.float32)
        * factor
    )
    key_grad = (
        jnp.einsum("bhqk,bqhd->bkhd", score_grad, queries, preferred_element_type=jnp.float32)
        * factor
    )
    value_grad = jnp.einsum(
        "bhqk,bqhd->bkhd",
        attn_probs.astype(jnp.bfloat16),
        mix_grad,
        preferred_element_type=jnp.float32,
    )
    return (query_grad, key_grad, value_grad)


def shards(flat_params, w_fc1, w_fc2, w_up, w_down, patches, clip_ids, visible_index, cotangent):
    w_qkv, w_proj, g_one, g_two, w_embed, mask_token, w_dqkv, w_dproj, gd_one, gd_two = unpack(
        flat_params
    )
    buffers = patches.shape[0] // VIS
    rows_here = cotangent.shape[0]
    head_size = D // HEADS
    visible = visible_index.reshape(buffers, VIS)
    segment = jnp.take_along_axis(clip_ids.reshape(buffers, ROWS), visible, axis=1)
    allowed = (segment[:, :, None] == segment[:, None, :])[:, None]
    inputs = patches.astype(jnp.float32)
    enc_norm, norm_pull1 = jax.vjp(layer_norm, inputs, g_one.astype(jnp.float32))
    enc_norm = enc_norm.astype(jnp.bfloat16)
    enc_qkv = (
        matmul(enc_norm, w_qkv).astype(jnp.bfloat16).reshape(buffers, VIS, 3, HEADS, head_size)
    )
    enc_query, enc_key, enc_value = (enc_qkv[:, :, 0], enc_qkv[:, :, 1], enc_qkv[:, :, 2])
    enc_out, enc_lse = attend_forward(enc_query, enc_key, enc_value, allowed)
    enc_mix = enc_out.reshape(-1, D).astype(jnp.bfloat16)
    first = inputs + matmul(enc_mix, w_proj)
    enc_in2, norm_pull2 = jax.vjp(layer_norm, first, g_two.astype(jnp.float32))
    enc_in2 = enc_in2.astype(jnp.bfloat16)
    enc_all = lax.all_gather(enc_in2, "mlp", axis=0, tiled=True)
    enc_act, gelu_pull1 = jax.vjp(exact_gelu, matmul(enc_all, w_fc1))
    enc_hidden = enc_act.astype(jnp.bfloat16)
    second = first + lax.psum_scatter(
        matmul(enc_hidden, w_fc2), "mlp", scatter_dimension=0, tiled=True
    )
    second_low = second.astype(jnp.bfloat16)
    embedded = matmul(second_low, w_embed).astype(jnp.bfloat16)
    matches = visible[:, None, :] == jnp.arange(ROWS, dtype=jnp.int32)[None, :, None]
    filled = jnp.einsum(
        "brv,bvd->brd",
        matches.astype(jnp.bfloat16),
        embedded.reshape(buffers, VIS, DD),
        preferred_element_type=jnp.float32,
    )
    masked_rows = 1.0 - jnp.any(matches, axis=2).astype(jnp.float32)
    start = (filled + masked_rows[:, :, None] * mask_token.astype(jnp.float32)).reshape(
        rows_here, DD
    )
    dec_norm, norm_pull3 = jax.vjp(layer_norm, start, gd_one.astype(jnp.float32))
    dec_norm = dec_norm.astype(jnp.bfloat16)
    dec_qkv = matmul(dec_norm, w_dqkv).astype(jnp.bfloat16)
    dec_query = to_windows(dec_qkv[:, :DD], DHEADS)
    dec_key = to_windows(dec_qkv[:, DD : 2 * DD], DHEADS)
    dec_value = to_windows(dec_qkv[:, 2 * DD :], DHEADS)
    dec_out, dec_lse = attend_forward(dec_query, dec_key, dec_value, None)
    dec_mix = from_windows(dec_out, buffers).astype(jnp.bfloat16)
    middle = start + matmul(dec_mix, w_dproj)
    dec_in2, norm_pull4 = jax.vjp(layer_norm, middle, gd_two.astype(jnp.float32))
    dec_in2 = dec_in2.astype(jnp.bfloat16)
    rows_all = lax.all_gather(dec_in2, "mlp", axis=0, tiled=True)
    dec_act, gelu_pull2 = jax.vjp(exact_gelu, matmul(rows_all, w_up))
    dec_hidden = dec_act.astype(jnp.bfloat16)
    decoded_full = middle + lax.psum_scatter(
        matmul(dec_hidden, w_down).astype(jnp.bfloat16), "mlp", scatter_dimension=0, tiled=True
    ).astype(jnp.float32)
    upstream_all = lax.all_gather(cotangent, "mlp", axis=0, tiled=True)
    down_grad_part = transposed(dec_hidden, upstream_all)
    pre_grad = gelu_pull2(against(upstream_all, w_down))[0].astype(jnp.bfloat16)
    up_grad_part = transposed(rows_all, pre_grad)
    in2_grad = lax.psum_scatter(
        against(pre_grad, w_up).astype(jnp.bfloat16), "mlp", scatter_dimension=0, tiled=True
    ).astype(jnp.float32)
    decoded = decoded_full.astype(jnp.bfloat16)
    middle_part, gd_two_grad = norm_pull4(in2_grad)
    middle_grad = cotangent.astype(jnp.float32) + middle_part
    dec_branch = middle_grad.astype(jnp.bfloat16)
    dproj_grad = transposed(dec_mix, dec_branch)
    dec_mix_grad = to_windows(against(dec_branch, w_dproj).astype(jnp.bfloat16), DHEADS)
    dq_grad, dk_grad, dv_grad = attend_backward(
        dec_query, dec_key, dec_value, None, dec_lse, dec_mix_grad
    )
    dec_qkv_grad = jnp.concatenate(
        [
            from_windows(dq_grad, buffers),
            from_windows(dk_grad, buffers),
            from_windows(dv_grad, buffers),
        ],
        axis=1,
    ).astype(jnp.bfloat16)
    dqkv_weight_grad = transposed(dec_norm, dec_qkv_grad)
    start_part, gd_one_grad = norm_pull3(against(dec_qkv_grad, w_dqkv))
    start_grad = (middle_grad + start_part).reshape(buffers, ROWS, DD)
    mask_grad = jnp.sum(start_grad * masked_rows[:, :, None], axis=(0, 1))
    embed_grad = (
        jnp.take_along_axis(start_grad, visible[:, :, None], axis=1)
        .reshape(-1, DD)
        .astype(jnp.bfloat16)
    )
    w_embed_grad = transposed(second_low, embed_grad)
    second_grad = against(embed_grad, w_embed)
    out_grad = second_grad.astype(jnp.bfloat16)
    out_all = lax.all_gather(out_grad, "mlp", axis=0, tiled=True)
    fc2_grad_part = transposed(enc_hidden, out_all)
    fc_pre_grad = gelu_pull1(against(out_all, w_fc2))[0].astype(jnp.bfloat16)
    fc1_grad_part = transposed(enc_all, fc_pre_grad)
    enc_in2_grad = lax.psum_scatter(
        against(fc_pre_grad, w_fc1).astype(jnp.bfloat16), "mlp", scatter_dimension=0, tiled=True
    ).astype(jnp.float32)
    first_part, g_two_grad = norm_pull2(enc_in2_grad)
    first_grad = second_grad + first_part
    enc_branch = first_grad.astype(jnp.bfloat16)
    proj_grad = transposed(enc_mix, enc_branch)
    enc_mix_grad = (
        against(enc_branch, w_proj).astype(jnp.bfloat16).reshape(buffers, VIS, HEADS, head_size)
    )
    eq_grad, ek_grad, ev_grad = attend_backward(
        enc_query, enc_key, enc_value, allowed, enc_lse, enc_mix_grad
    )
    enc_qkv_grad = (
        jnp.stack([eq_grad, ek_grad, ev_grad], axis=2).reshape(-1, 3 * D).astype(jnp.bfloat16)
    )
    qkv_weight_grad = transposed(enc_norm, enc_qkv_grad)
    input_part, g_one_grad = norm_pull1(against(enc_qkv_grad, w_qkv))
    input_grad = first_grad + input_part
    members = [
        qkv_weight_grad,
        proj_grad,
        g_one_grad,
        g_two_grad,
        w_embed_grad,
        mask_grad,
        dqkv_weight_grad,
        dproj_grad,
        gd_one_grad,
        gd_two_grad,
    ]
    flat_grad = jnp.concatenate(
        [member.reshape(-1) for member in members]
        + [jnp.zeros((flat_params.shape[0] - PARAMS,), jnp.float32)]
    )
    shard_grad = lax.psum_scatter(
        flat_grad.astype(jnp.bfloat16), "mlp", scatter_dimension=0, tiled=True
    )
    param_grad, fc1_grad, fc2_grad, up_grad, down_grad = (
        lax.psum(shard_grad, "clips").astype(jnp.float32),
        lax.psum(fc1_grad_part.astype(jnp.bfloat16), "clips").astype(jnp.float32),
        lax.psum(fc2_grad_part.astype(jnp.bfloat16), "clips").astype(jnp.float32),
        lax.psum(up_grad_part.astype(jnp.bfloat16), "clips").astype(jnp.float32),
        lax.psum(down_grad_part.astype(jnp.bfloat16), "clips").astype(jnp.float32),
    )
    return (decoded, input_grad, param_grad, fc1_grad, fc2_grad, up_grad, down_grad)


def solution(mesh):
    placed = (
        P(),
        P(None, "mlp"),
        P("mlp", None),
        P(None, "mlp"),
        P("mlp", None),
        P(("clips", "mlp"), None),
        P(("clips", "mlp")),
        P(("clips", "mlp")),
        P(("clips", "mlp"), None),
    )
    return jax.shard_map(
        shards,
        mesh=mesh,
        in_specs=placed,
        out_specs=(
            P(("clips", "mlp"), None),
            P(("clips", "mlp"), None),
            P("mlp"),
            P(None, "mlp"),
            P("mlp", None),
            P(None, "mlp"),
            P("mlp", None),
        ),
        check_vma=False,
    )
```

profile of v0, /device:TPU:0, one launch (start us, length us, event | category | flops | bytes accessed | tf_op | source)
XLA Modules:
  0.0 1081.5 jit_solution(7096899038210828048)
XLA Ops:
  44.2 14.8 %all_gather.12 = bf16[624,768]{1,0:T(8,128)(2,1)S(1)} all-gather(bf16[312,768]{1,0:T(8,128)(2,1)S(1)} %multiply_convert_fusion.8), channel_id=1, replica_groups=mesh['clips'=16,'mlp'=2] {'mlp'}, dimensions={0}, use_global_device_ids=true | all-gather | bytes 1437696 | tf_op jit(solution)/shard_map/all_gather | solution.py:140
  59.0 11.4 %multiply_convert_fusion.5 = (bf16[624,1536]{1,0:T(8,128)(2,1)S(1)}, f32[624,1536]{1,0:T(8,128)}, f32[624,1536]{1,0:T(8,128)}) fusion(bf16[624,768]{1,0:T(8,128)(2,1)S(1)} %all_gather.12, bf16[768,1536]{1,0:T(8,128)(2,1)S(1)} %copy-done), kind=kOutput, calls=%fused_computation.60 | convolution fusion | flops 1534500864 | bytes 12902400 | tf_op jit(solution)/shard_map/dot_general | solution.py:56
  91.3 14.7 %reduce-scatter.5.cloned.1.call-done = f32[312,768]{1,0:T(8,128)} async-done(((f32[624,768]{1,0:T(8,128)}), f32[312,768]{1,0:T(8,128)}) %reduce-scatter.5.cloned.1.call-update) | async-done | bytes 958480 | tf_op jit(solution)/shard_map/reduce_scatter | solution.py:143
  147.9 9.1 copy.126
  165.0 9.1 copy.124
  174.0 12.6 %multiply_reduce_fusion.1 = (f32[96,16,16]{2,1,0:T(8,128)S(1)}, f32[96,16,16,16]{2,3,1,0:T(8,128)}) fusion(bf16[96,16,16,32]{3,1,2,0:T(8,128)(2,1)} %bitcast.143, bf16[96,16,16,32]{3,1,2,0:T(8,128)(2,1)} %bitcast.139), kind=kOutput, calls=%fused_computation.27 | convolution fusion | flops 25927680 | bytes 4816896 | tf_op jit(solution)/shard_map/bqhd,bkhd->bhqk/dot_general | solution.py:74
  194.1 10.4 convert_bitcast_fusion.1
  212.5 9.1 convert_element_type.229
  236.0 44.3 %all-gather.3.cloned.1.call-done = bf16[3072,512]{0,1:T(8,128)(2,1)} async-done(((bf16[1536,512]{0,1:T(8,128)(2,1)}), bf16[3072,512]{0,1:T(8,128)(2,1)}) %all-gather.3.cloned.1.call-update) | async-done | bytes 3145744 | tf_op jit(solution)/shard_map/all_gather | solution.py:170
  280.4 33.5 %multiply_convert_fusion.3 = (bf16[3072,1024]{1,0:T(8,128)(2,1)}, f32[3072,1024]{1,0:T(8,128)}, f32[3072,1024]{1,0:T(8,128)}) fusion(bf16[3072,512]{0,1:T(8,128)(2,1)} %all-gather.3.cloned.1.call-done, bf16[512,1024]{1,0:T(8,128)(2,1)} %param.12), kind=kOutput, calls=%fused_computation.10 | convolution fusion | flops 3425697792 | bytes 35651584 | tf_op jit(solution)/shard_map/dot_general | solution.py:56
  313.9 13.0 %all-gather.5.cloned.1.call-done = bf16[3072,512]{1,0:T(8,128)(2,1)} async-done(((bf16[1536,512]{1,0:T(8,128)(2,1)}), bf16[3072,512]{1,0:T(8,128)(2,1)}) %all-gather.5.cloned.1.call-update) | async-done | bytes 3145744 | tf_op jit(solution)/shard_map/all_gather | solution.py:176
  326.9 14.1 %add_convert_fusion = bf16[3072,1024]{1,0:T(8,128)(2,1)S(1)} fusion(f32[3072,1024]{1,0:T(8,128)} %get-tuple-element.58, f32[3072,1024]{1,0:T(8,128)} %get-tuple-element.83, bf16[3072,512]{1,0:T(8,128)(2,1)} %all-gather.5.cloned.1.call-done, bf16[1024,512]{1,0:T(8,128)(2,1)} %param.13), kind=kOutput, calls=%fused_computation.9 | convolution fusion | flops 3265265664 | bytes 35651584 | tf_op jit(solution)/shard_map/dot_general | solution.py:66
  352.8 9.2 convolution_convert_fusion.3
  362.1 29.9 %reduce-scatter.9.cloned.1.call-done = bf16[1536,512]{0,1:T(8,128)(2,1)} async-done(((bf16[3072,512]{0,1:T(8,128)(2,1)}), bf16[1536,512]{0,1:T(8,128)(2,1)}) %reduce-scatter.9.cloned.1.call-update) | async-done | bytes 1572880 | tf_op jit(solution)/shard_map/reduce_scatter | solution.py:180
  415.4 10.5 convert_bitcast_fusion
  433.9 9.1 reshape.607
  449.9 14.4 %multiply_reduce_fusion = (f32[96,16,16]{2,1,0:T(8,128)}, f32[96,16,16,16]{2,3,1,0:T(8,128)}) fusion(f32[96,16,16,16]{2,3,1,0:T(8,128)} %get-tuple-element.80, f32[96,16,16]{2,1,0:T(8,128)S(1)} %log_add_fusion, bf16[96,16,16,32]{3,1,2,0:T(8,128)(2,1)} %bitcast.146, bf16[96,16,16,32]{3,2,1,0:T(8,128)(2,1)} %bitcast.142), kind=kOutput, calls=%fused_computation.7 | convolution fusion | flops 26714112 | bytes 6488064 | tf_op jit(solution)/shard_map/bqhd,bkhd->bhqk/dot_general | solution.py:95
  464.4 10.1 multiply_convert_fusion.2
  488.3 9.1 reshape.605
  515.8 9.1 reshape.603
  556.0 13.4 %all_gather.15 = bf16[624,768]{1,0:T(8,128)(2,1)S(1)} all-gather(bf16[312,768]{1,0:T(8,128)(2,1)S(1)} %get-tuple-element.88), channel_id=1, replica_groups=mesh['clips'=16,'mlp'=2] {'mlp'}, dimensions={0}, use_global_device_ids=true | all-gather | bytes 1437696 | tf_op jit(solution)/shard_map/all_gather | solution.py:212
  645.5 13.4 %dynamic-update-slice.4 = bf16[3804160]{0:T(1024)(128)(2,1)} dynamic-update-slice(bf16[3804160]{0:T(1024)(128)(2,1)} %dynamic-update-slice.3, bf16[393216]{0:T(1024)(128)(2,1)} %bitcast.162, s32[]{} %constant.44) | dynamic-update-slice | bytes 1572868
  691.6 157.8 %all-reduce.5.cloned.1.call-done = bf16[3804160]{0:T(1024)(128)(2,1)} async-done(((bf16[3804160]{0:T(1024)(128)(2,1)}), bf16[3804160]{0:T(1024)(128)(2,1)}) %all-reduce.5.cloned.1.call-update) | async-done | bytes 7608336
  859.5 201.2 %all-reduce.7.cloned.1.call-done = (bf16[1902080]{0:T(1024)(128)(2,1)}, bf16[768,1536]{1,0:T(8,128)(2,1)}, bf16[1536,768]{1,0:T(8,128)(2,1)}, bf16[512,1024]{1,0:T(8,128)(2,1)}, bf16[1024,512]{1,0:T(8,128)(2,1)}) async-done(((bf16[1902080]{0:T(1024)(128)(2,1)}, bf16[768,1536]{1,0:T(8,128)(2,1)}, bf16[1536,768]{1,0:T(8,128)(2,1)}, bf16[512,1024]{1,0:T(8,128)(2,1)}, bf16[1024,512]{1,0:T(8,128)(2,1)}), ...) | async-done | bytes 10619920 | tf_op jit(solution)/shard_map/psum | solution.py:255
  (335 shorter events, 382.3 us)
Async XLA Ops:
  7.2 51.8 %copy-start = (bf16[768,1536]{1,0:T(8,128)(2,1)S(1)}, bf16[768,1536]{1,0:T(8,128)(2,1)}, u32[]{:S(2)}) copy-start(bf16[768,1536]{1,0:T(8,128)(2,1)} %param.10) | copy-start | bytes 7077892
  7.2 98.9 %reduce-scatter.5.cloned.1.call-start = ((), (), s32[]{:S(2)}) async-start(), calls=%async_computation.4 | async-start | bytes 2875392 | tf_op jit(solution)/shard_map/reduce_scatter | solution.py:143
  8.1 11.5 %copy-start.56 = (f32[768]{0:T(1024)}, f32[768]{0:T(1024)S(1)}, u32[]{:S(2)}) copy-start(f32[768]{0:T(1024)S(1)} %get-tuple-element.67) | copy-start | bytes 9220
  8.1 35.9 %copy-start.46 = (f32[768]{0:T(1024)}, f32[768]{0:T(1024)S(1)}, u32[]{:S(2)}) copy-start(f32[768]{0:T(1024)S(1)} %get-tuple-element.66) | copy-start | bytes 9220
  11.7 12.4 %copy-start.58 = (f32[312]{0:T(512)}, f32[312]{0:T(512)S(1)}, u32[]{:S(2)}) copy-start(f32[312]{0:T(512)S(1)} %broadcast_multiply_fusion.3) | copy-start | bytes 3748
  12.0 12.1 %copy-start.68 = (f32[312]{0:T(512)}, f32[312]{0:T(512)S(1)}, u32[]{:S(2)}) copy-start(f32[312]{0:T(512)S(1)} %fusion.61) | copy-start | bytes 3748
  12.0 12.1 %copy-start.66 = (f32[312]{0:T(512)}, f32[312]{0:T(512)S(1)}, u32[]{:S(2)}) copy-start(f32[312]{0:T(512)S(1)} %fusion.68) | copy-start | bytes 3748
  43.7 62.4 %copy-start.8 = (f32[312,768]{1,0:T(8,128)}, f32[312,768]{1,0:T(8,128)S(1)}, u32[]{:S(2)}) copy-start(f32[312,768]{1,0:T(8,128)S(1)} %get-tuple-element.75) | copy-start | bytes 2875396
  43.7 26.7 %copy-start.50 = (f32[312]{0:T(512)}, f32[312]{0:T(512)S(1)}, u32[]{:S(2)}) copy-start(f32[312]{0:T(512)S(1)} %broadcast_multiply_fusion.2) | copy-start | bytes 3748
  44.0 26.4 %copy-start.70 = (f32[312]{0:T(512)}, f32[312]{0:T(512)S(1)}, u32[]{:S(2)}) copy-start(f32[312]{0:T(512)S(1)} %multiply_reduce_fusion.8) | copy-start | bytes 3748
  44.0 26.4 %copy-start.60 = (f32[312]{0:T(512)}, f32[312]{0:T(512)S(1)}, u32[]{:S(2)}) copy-start(f32[312]{0:T(512)S(1)} %fusion.69) | copy-start | bytes 3748
  59.0 12.7 %copy-start.77 = (bf16[1536,768]{1,0:T(8,128)(2,1)S(1)}, bf16[1536,768]{1,0:T(8,128)(2,1)}, u32[]{:S(2)}) copy-start(bf16[1536,768]{1,0:T(8,128)(2,1)} %param.11) | copy-start | bytes 7077892
  74.6 205.8 %all-gather.3.cloned.1.call-start = ((), (), s32[]{:S(2)}) async-start(), calls=%async_computation.5 | async-start | bytes 4718592 | tf_op jit(solution)/shard_map/all_gather | solution.py:170
  91.3 24.0 %copy-start.64 = (f32[512]{0:T(512)}, f32[512]{0:T(512)S(1)}, u32[]{:S(2)}) copy-start(f32[512]{0:T(512)S(1)} %get-tuple-element.64) | copy-start | bytes 6148
  91.3 21.2 %copy-start.62 = (f32[1536]{0:T(1024)}, f32[1536]{0:T(1024)S(1)}, u32[]{:S(2)}) copy-start(f32[1536]{0:T(1024)S(1)} %convert_subtract_fusion.1) | copy-start | bytes 18436
  235.3 91.6 %all-gather.5.cloned.1.call-start = ((), (), s32[]{:S(2)}) async-start(), calls=%async_computation.7 | async-start | bytes 4718592 | tf_op jit(solution)/shard_map/all_gather | solution.py:176
  236.0 156.0 %reduce-scatter.9.cloned.1.call-start = ((), (), s32[]{:S(2)}) async-start(), calls=%async_computation.8 | async-start | bytes 4718592 | tf_op jit(solution)/shard_map/reduce_scatter | solution.py:180
  326.9 16.8 %copy-start.79 = (bf16[512,1024]{1,0:T(8,128)(2,1)S(1)}, bf16[512,1024]{1,0:T(8,128)(2,1)}, u32[]{:S(2)}) copy-start(bf16[512,1024]{1,0:T(8,128)(2,1)} %param.12) | copy-start | bytes 3145732
  348.5 192.1 %reduce-scatter.7.cloned.1.call-start = ((), (), s32[]{:S(2)}) async-start(), calls=%async_computation.6 | async-start | bytes 4718592 | tf_op jit(solution)/shard_map/reduce_scatter | solution.py:173
  362.0 237.0 %reduce-scatter.11.cloned.1.call-start = ((), (), s32[]{:S(2)}) async-start(), calls=%async_computation.9 | async-start | bytes 1437696 | tf_op jit(solution)/shard_map/reduce_scatter | solution.py:216
  554.6 14.8 %copy-start.78 = (bf16[1536,768]{1,0:T(8,128)(2,1)S(1)}, bf16[1536,768]{1,0:T(8,128)(2,1)}, u32[]{:S(2)}) copy-start(bf16[1536,768]{1,0:T(8,128)(2,1)} %param.11) | copy-start | bytes 7077892
  579.5 269.9 %all-reduce.5.cloned.1.call-start = ((), (), s32[]{:S(2)}) async-start(), calls=%async_computation.10 | async-start | bytes 15216640
  579.6 11.6 %copy-start.41 = (bf16[312,768]{1,0:T(8,128)(2,1)S(1)}, bf16[312,768]{1,0:T(8,128)(2,1)}, u32[]{:S(2)}) copy-start(bf16[312,768]{1,0:T(8,128)(2,1)} %add_convert_fusion.3) | copy-start | bytes 1437700
  667.6 393.1 %all-reduce.7.cloned.1.call-start = ((), (), s32[]{:S(2)}) async-start(), calls=%async_computation.11 | async-start | bytes 21241856 | tf_op jit(solution)/shard_map/psum | solution.py:255
  (73 other events, 307.1 us)
Sparse Core Ops, SparseCore 0:
  74.7 31.3 reduce-scatter.4
  235.4 44.9 all-gather.2
  281.9 44.9 all-gather.4
  348.6 43.3 reduce-scatter.8
  394.2 43.3 reduce-scatter.6
  579.6 19.3 reduce-scatter.10
  667.7 181.6 all-reduce.4
  854.4 206.2 all-reduce.6
where the time goes:
time: 1090 us; the launch traced here: 1080 us
  waiting for transfers between devices  464 us (43%)
  local copies, waits for them, and re-layouts  275 us (25%)
  matrix products  229 us (21%)
  other arithmetic  69.1 us (6%)
  blocking collectives  28.1 us (3%)
  between operations  16.1 us (1%)
    psum x1, waiting for transfers between devices, shards(): lax.psum(shard_grad, 'clips').astype(jnp.float32)  201 us
    unnamed x9, waiting for transfers between devices  159 us
    dot_general x8, matrix products, matmul(): return jnp.dot(left, right, preferred_element_type=jnp.float32)  72.3 us
    unnamed x193, local copies, waits for them, and re-layouts  59.8 us
    all_gather x1, waiting for transfers between devices, shards(): rows_all = lax.all_gather(dec_in2, 'mlp', axis=0, tiled=True)  44.3 us
    dot_general x9, matrix products, transposed(): lax.dot_general(left, right, (((0,), (0,)), ((), ())), preferred_element_...  39.4 us
    dot_general x9, matrix products, against(): lax.dot_general(left, right, (((1,), (1,)), ((), ())), preferred_element_...  37.4 us
    reshape x4, local copies, waits for them, and re-layouts, to_windows(): source.reshape(-1, LONG_FRAMES // WIN, WIN, FREQ // WIN, WIN, head_count,...  32.4 us
  transfers between devices with their start and end apart: 8, of which 7 were waited for; matrix products, arithmetic and copies ran while one was open for 23% of the time, Pallas kernels for 0%

commit v1 on v0

--- a/solution.py
+++ b/solution.py
@@ -252,7 +252,7 @@
         flat_grad.astype(jnp.bfloat16), "mlp", scatter_dimension=0, tiled=True
     )
     param_grad, fc1_grad, fc2_grad, up_grad, down_grad = (
-        lax.psum(shard_grad, "clips").astype(jnp.float32),
+        jnp.sum(lax.all_gather(shard_grad, "clips"), axis=0).astype(jnp.float32),
         lax.psum(fc1_grad_part.astype(jnp.bfloat16), "clips").astype(jnp.float32),
         lax.psum(fc2_grad_part.astype(jnp.bfloat16), "clips").astype(jnp.float32),
         lax.psum(up_grad_part.astype(jnp.bfloat16), "clips").astype(jnp.float32),

time: 1090 us -> 2240 us (2.06)
  other arithmetic: 69.1 us -> 703 us
  waiting for transfers between devices: 464 us -> 935 us
  local copies, waits for them, and re-layouts: 275 us -> 320 us
    reduce_sum x0 -> x1, other arithmetic: none -> 632 us  [shards(): jnp.sum(lax.all_gather(shard_grad, 'clips'), axis=0).astype(jnp.float32)]
    all_gather x0 -> x1, waiting for transfers between devices: none -> 573 us  [shards(): lax.all_gather(shard_grad, 'clips')]
    psum x1, waiting for transfers between devices: 201 us -> 101 us  [shards(): lax.psum(fc1_grad_part.astype(jnp.bfloat16), 'clips').astype(jnp.float32)]
    unnamed x193 -> x200, local copies, waits for them, and re-layouts: 59.8 us -> 100 us
    unnamed x9 -> x10, waiting for transfers between devices: 159 us -> 158 us
  transfers between devices with their start and end apart: 8 -> 9, of which waited for: 7 -> 8; matrix products, arithmetic and copies ran while one was open for 23% -> 14% of each run, Pallas kernels for 0% -> 0%
where the time goes in v1:
time: 2240 us; the launch traced here: 2230 us
  waiting for transfers between devices  935 us (42%)
  other arithmetic  703 us (31%)
  local copies, waits for them, and re-layouts  320 us (14%)
  matrix products  230 us (10%)
  blocking collectives  28.5 us (1%)
    reduce_sum x1, other arithmetic, shards(): jnp.sum(lax.all_gather(shard_grad, 'clips'), axis=0).astype(jnp.float32)  632 us
    all_gather x1, waiting for transfers between devices, shards(): lax.all_gather(shard_grad, 'clips')  573 us
    unnamed x10, waiting for transfers between devices  158 us
    psum x1, waiting for transfers between devices, shards(): lax.psum(fc1_grad_part.astype(jnp.bfloat16), 'clips').astype(jnp.float32)  101 us
    unnamed x200, local copies, waits for them, and re-layouts  100 us
    dot_general x8, matrix products, matmul(): return jnp.dot(left, right, preferred_element_type=jnp.float32)  71 us
  transfers between devices with their start and end apart: 9, of which 8 were waited for; matrix products, arithmetic and copies ran while one was open for 14% of the time, Pallas kernels for 0%

profile of v1, /device:TPU:0, one launch (start us, length us, event | category | flops | bytes accessed | tf_op | source)
XLA Modules:
  0.0 2232.4 jit_solution(11222896757157623585)
XLA Ops:
  45.5 15.1 all_gather.18
  60.6 11.4 multiply_convert_fusion.5
  93.0 14.7 reduce-scatter.5.cloned.1.call-done
  175.6 12.6 multiply_reduce_fusion.1
  195.7 10.2 convert_bitcast_fusion.1
  237.4 44.3 %all-gather.6.cloned.1.call-done = bf16[3072,512]{0,1:T(8,128)(2,1)} async-done(((bf16[1536,512]{0,1:T(8,128)(2,1)}), bf16[3072,512]{0,1:T(8,128)(2,1)}) %all-gather.6.cloned.1.call-update) | async-done | bytes 3145744 | tf_op jit(solution)/shard_map/all_gather | solution.py:170
  281.7 33.8 %multiply_convert_fusion.3 = (bf16[3072,1024]{1,0:T(8,128)(2,1)}, f32[3072,1024]{1,0:T(8,128)}, f32[3072,1024]{1,0:T(8,128)}) fusion(bf16[3072,512]{0,1:T(8,128)(2,1)} %all-gather.6.cloned.1.call-done, bf16[512,1024]{1,0:T(8,128)(2,1)} %param.12), kind=kOutput, calls=%fused_computation.10 | convolution fusion | flops 3425697792 | bytes 35651584 | tf_op jit(solution)/shard_map/dot_general | solution.py:56
  315.5 12.7 all-gather.8.cloned.1.call-done
  328.2 14.1 add_convert_fusion
  354.1 9.2 convolution_convert_fusion.3
  363.4 29.9 %reduce-scatter.9.cloned.1.call-done = bf16[1536,512]{0,1:T(8,128)(2,1)} async-done(((bf16[3072,512]{0,1:T(8,128)(2,1)}), bf16[1536,512]{0,1:T(8,128)(2,1)}) %reduce-scatter.9.cloned.1.call-update) | async-done | bytes 1572880 | tf_op jit(solution)/shard_map/reduce_scatter | solution.py:180
  416.6 10.5 convert_bitcast_fusion
  435.1 9.1 reshape.607
  451.1 14.4 multiply_reduce_fusion
  465.5 10.3 multiply_convert_fusion.2
  487.9 9.1 reshape.603
  517.4 9.1 reshape.605
  557.8 13.4 all_gather.21
  647.1 13.4 dynamic-update-slice.4
  692.7 157.3 %all-reduce.5.cloned.1.call-done = bf16[3804160]{0:T(1024)(128)(2,1)} async-done(((bf16[3804160]{0:T(1024)(128)(2,1)}), bf16[3804160]{0:T(1024)(128)(2,1)}) %all-reduce.5.cloned.1.call-update) | async-done | bytes 7608336
  853.6 44.2 %reshape.643 = bf16[1,1,1902080]{2,1,0:T(2,128)(2,1)} reshape(bf16[1902080]{0:T(1024)(128)(2,1)S(1)} %dynamic-slice.1) | data formatting | bytes 7608320
  903.2 100.5 %all-reduce.7.cloned.1.call-done = (bf16[768,1536]{1,0:T(8,128)(2,1)}, bf16[1536,768]{1,0:T(8,128)(2,1)}, bf16[512,1024]{1,0:T(8,128)(2,1)}, bf16[1024,512]{1,0:T(8,128)(2,1)}) async-done(((bf16[768,1536]{1,0:T(8,128)(2,1)}, bf16[1536,768]{1,0:T(8,128)(2,1)}, bf16[512,1024]{1,0:T(8,128)(2,1)}, bf16[1024,512]{1,0:T(8,128)(2,1)}), (bf16[768,1536]{1,0:T(8,128)(2,1)}, bf16[1536,768]{1,0:T(8,128)(2,1)}, ...) | async-done | bytes 6815760 | tf_op jit(solution)/shard_map/psum | solution.py:256
  1015.8 573.3 %all-gather.10.cloned.1.call-done = bf16[16,1,1902080]{2,1,0:T(2,128)(2,1)} async-done(((bf16[1,1,1902080]{2,1,0:T(2,128)(2,1)}), bf16[16,1,1902080]{2,1,0:T(2,128)(2,1)}) %all-gather.10.cloned.1.call-update) | async-done | bytes 60866576 | tf_op jit(solution)/shard_map/all_gather | solution.py:255
  1589.1 631.6 %reduce_sum.310 = bf16[1902080]{0:T(1024)(128)(2,1)} reduce(bf16[16,1,1902080]{2,1,0:T(2,128)(2,1)} %all-gather.10.cloned.1.call-done, bf16[]{:T(256)} %constant.91.clone.1), dimensions={0,1}, to_apply=%region_33.34 | reduce | flops 28531200 | bytes 64670720 | tf_op jit(solution)/shard_map/reduce_sum | solution.py:255
  (345 shorter events, 412.5 us)
Async XLA Ops:
  7.2 53.4 %copy-start = (bf16[768,1536]{1,0:T(8,128)(2,1)S(1)}, bf16[768,1536]{1,0:T(8,128)(2,1)}, u32[]{:S(2)}) copy-start(bf16[768,1536]{1,0:T(8,128)(2,1)} %param.10) | copy-start | bytes 7077892
  7.2 100.5 %reduce-scatter.5.cloned.1.call-start = ((), (), s32[]{:S(2)}) async-start(), calls=%async_computation.4 | async-start | bytes 2875392 | tf_op jit(solution)/shard_map/reduce_scatter | solution.py:143
  8.1 20.7 copy-start.59
  8.1 36.9 %copy-start.49 = (f32[768]{0:T(1024)}, f32[768]{0:T(1024)S(1)}, u32[]{:S(2)}) copy-start(f32[768]{0:T(1024)S(1)} %get-tuple-element.65) | copy-start | bytes 9220
  13.9 14.9 copy-start.76
  16.9 12.0 copy-start.61
  43.3 28.7 %copy-start.32 = (bf16[12,64,312]{2,1,0:T(8,128)(2,1)}, bf16[12,64,312]{2,1,0:T(8,128)(2,1)S(1)}, u32[]{:S(2)}) copy-start(bf16[12,64,312]{2,1,0:T(8,128)(2,1)S(1)} %fusion.49) | copy-start | bytes 1437700
  44.0 63.6 %copy-start.9 = (f32[312,768]{1,0:T(8,128)}, f32[312,768]{1,0:T(8,128)S(1)}, u32[]{:S(2)}) copy-start(f32[312,768]{1,0:T(8,128)S(1)} %get-tuple-element.74) | copy-start | bytes 2875396
  60.6 11.4 copy-start.40
  60.6 12.7 copy-start.80
  76.2 205.5 %all-gather.6.cloned.1.call-start = ((), (), s32[]{:S(2)}) async-start(), calls=%async_computation.5 | async-start | bytes 4718592 | tf_op jit(solution)/shard_map/all_gather | solution.py:170
  92.9 24.0 %copy-start.67 = (f32[512]{0:T(512)}, f32[512]{0:T(512)S(1)}, u32[]{:S(2)}) copy-start(f32[512]{0:T(512)S(1)} %get-tuple-element.63) | copy-start | bytes 6148
  92.9 21.1 copy-start.65
  236.6 91.6 %all-gather.8.cloned.1.call-start = ((), (), s32[]{:S(2)}) async-start(), calls=%async_computation.7 | async-start | bytes 4718592 | tf_op jit(solution)/shard_map/all_gather | solution.py:176
  237.4 156.0 %reduce-scatter.9.cloned.1.call-start = ((), (), s32[]{:S(2)}) async-start(), calls=%async_computation.8 | async-start | bytes 4718592 | tf_op jit(solution)/shard_map/reduce_scatter | solution.py:180
  328.2 16.8 copy-start.82
  349.8 192.3 %reduce-scatter.7.cloned.1.call-start = ((), (), s32[]{:S(2)}) async-start(), calls=%async_computation.6 | async-start | bytes 4718592 | tf_op jit(solution)/shard_map/reduce_scatter | solution.py:173
  363.4 237.5 %reduce-scatter.11.cloned.1.call-start = ((), (), s32[]{:S(2)}) async-start(), calls=%async_computation.9 | async-start | bytes 1437696 | tf_op jit(solution)/shard_map/reduce_scatter | solution.py:216
  556.4 21.0 copy-start.39
  556.4 14.8 copy-start.81
  581.3 268.7 %all-reduce.5.cloned.1.call-start = ((), (), s32[]{:S(2)}) async-start(), calls=%async_computation.11 | async-start | bytes 15216640
  643.2 21.4 copy-start.36
  668.1 335.6 %all-reduce.7.cloned.1.call-start = ((), (), s32[]{:S(2)}) async-start(), calls=%async_computation.12 | async-start | bytes 13631488 | tf_op jit(solution)/shard_map/psum | solution.py:256
  690.9 898.3 %all-gather.10.cloned.1.call-start = ((), (), s32[]{:S(2)}) async-start(), calls=%async_computation.10 | async-start | bytes 129341440 | tf_op jit(solution)/shard_map/all_gather | solution.py:255
  (76 other events, 326.9 us)
Sparse Core Ops, SparseCore 0:
  76.3 31.3 reduce-scatter.4
  236.7 44.8 all-gather.5
  283.2 44.9 all-gather.7
  350.0 43.3 reduce-scatter.8
  395.5 43.3 reduce-scatter.6
  581.4 19.3 reduce-scatter.10
  668.2 181.6 all-reduce.4
  854.6 149.0 all-reduce.6
  1005.9 583.1 all-gather.9
